TPU v7x, 32 devices: a whole 2x2x4 slice. The times are simulated.
32 devices in a mesh: fsdp: 8 (over y, x, core), sp: 4 (over z).
Axes of the slice: x: 2, y: 2, z: 4, core: 2. Of those that a mesh axis runs over, the one named last changes fastest.
Arguments:
- hidden_in: bfloat16 [8, 1024, 2048], P('fsdp', 'sp'), may hold values from -6 to 6
- segments: int32 [8, 1024], P('fsdp'), may hold values from 0 to 3, never falling along the last dimension, each value on 1 to 640 neighbouring positions
- ln1_gain: float32 [2048], replicated, may hold values from 0.5 to 1.5
- ln1_bias: float32 [2048], replicated, may hold values from -1 to 1
- ln2_gain: float32 [2048], replicated, may hold values from 0.5 to 1.5
- ln2_bias: float32 [2048], replicated, may hold values from -1 to 1
- w_qkv: bfloat16 [6144, 2048], P('fsdp'), may hold values from -0.125 to 0.125
- b_qkv: float32 [6144], replicated, may hold values from -1 to 1
- w_dense: bfloat16 [2048, 2048], P('fsdp'), may hold values from -0.75 to 0.75
- b_dense: float32 [2048], replicated, may hold values from -1 to 1
- w_up: bfloat16 [8192, 2048], P('fsdp'), may hold values from -0.125 to 0.125
- b_up: float32 [8192], replicated, may hold values from -1 to 1
- w_down: bfloat16 [8192, 2048], P('fsdp'), may hold values from -0.0625 to 0.0625
- b_down: float32 [2048], replicated, may hold values from -1 to 1
- cotangent: bfloat16 [8, 1024, 2048], P('fsdp', 'sp'), may hold values from -6 to 6
Outputs:
- output: bfloat16 [8, 1024, 2048], P('fsdp', 'sp')
- input_grad: bfloat16 [8, 1024, 2048], P('fsdp', 'sp')
- grad_ln1_gain: float32 [2048], P('fsdp')
- grad_ln1_bias: float32 [2048], P('fsdp')
- grad_ln2_gain: float32 [2048], P('fsdp')
- grad_ln2_bias: float32 [2048], P('fsdp')
- grad_w_qkv: float32 [6144, 2048], P('fsdp')
- grad_b_qkv: float32 [6144], P('fsdp')
- grad_w_dense: float32 [2048, 2048], P('fsdp')
- grad_b_dense: float32 [2048], P('fsdp')
- grad_w_up: float32 [8192, 2048], P('fsdp')
- grad_b_up: float32 [8192], P('fsdp')
- grad_w_down: float32 [8192, 2048], P('fsdp')
- grad_b_down: float32 [2048], P('fsdp')
Inputs may be any that keep to these rules, and one draw needn't show every extreme that they name: `segments`: along each sequence the segment numbers never fall; each document is one run of 1 to 640 positions, and some document has exactly 640.
All inputs are finite; a program needn't handle non-finite values.
Results may differ from a plain program's by a relative error of at most 0.011.
Values may be sent and summed in bfloat16 or wider, within the bound.
A program may use at most 704 MiB of HBM per device.

v0:
```python
import math
import jax
import jax.numpy as jnp
from jax import lax
from jax.sharding import PartitionSpec as P

HEADS = 8
HEAD_DIM = 256
ROT = 64
EPSILON = 1e-05
NEGATIVE = -1e30
ROOT_HALF = 0.7071067811865476
ROOT_TWO_PI = 2.5066282746310002
SCALE = 1.0 / math.sqrt(HEAD_DIM)


def rounded(array):
    return lax.reduce_precision(array.astype(jnp.float32), 8, 7).astype(jnp.bfloat16)


def contract_rows(former, latter):
    return lax.dot_general(
        former, latter, (((0,), (0,)), ((), ())), preferred_element_type=jnp.float32
    )


def times_transposed(former, latter):
    return lax.dot_general(
        former, latter, (((1,), (1,)), ((), ())), preferred_element_type=jnp.float32
    )


def times(former, latter):
    return jnp.dot(former, latter, preferred_element_type=jnp.float32)


def norm_scaled(inputs):
    average = jnp.mean(inputs, axis=-1, keepdims=True)
    centred = inputs - average
    variance = jnp.mean(centred * centred, axis=-1, keepdims=True)
    inverse = lax.rsqrt(variance + EPSILON)
    return (centred * inverse, inverse)


def gelu_pair(hidden):
    cumulative = 0.5 * (1.0 + jax.scipy.special.erf(hidden * ROOT_HALF))
    return (
        hidden * cumulative,
        cumulative + hidden * jnp.exp(-0.5 * hidden * hidden) / ROOT_TWO_PI,
    )


def rotary_tables(segment_rows):
    length = segment_rows.shape[-1]
    places = jnp.arange(length, dtype=jnp.int32)
    changes = jnp.concatenate(
        [
            jnp.ones_like(segment_rows[..., :1]),
            (segment_rows[..., 1:] != segment_rows[..., :-1]).astype(jnp.int32),
        ],
        axis=-1,
    )
    first_place = lax.cummax(changes * places, axis=segment_rows.ndim - 1)
    position = (places - first_place).astype(jnp.float32)
    exponent = jnp.arange(0, ROT, 2).astype(jnp.float32) / ROT
    frequency = 1.0 / jnp.power(10000.0, exponent)
    angles = position[..., None] * frequency
    angles = jnp.concatenate([angles, angles], axis=-1)
    return (jnp.cos(angles), jnp.sin(angles))


def rotate(heads_part, cos_table, sin_table):
    half_rot = ROT // 2
    turned = heads_part[..., :ROT]
    swapped = jnp.concatenate([-turned[..., half_rot:], turned[..., :half_rot]], axis=-1)
    turned = turned * cos_table[..., None, :] + swapped * sin_table[..., None, :]
    return jnp.concatenate([turned, heads_part[..., ROT:]], axis=-1)


def unrotate(grads_part, cos_table, sin_table):
    half_rot = ROT // 2
    turned = grads_part[..., :ROT]
    along_sin = turned * sin_table[..., None, :]
    back_turn = jnp.concatenate([along_sin[..., half_rot:], -along_sin[..., :half_rot]], axis=-1)
    turned = turned * cos_table[..., None, :] + back_turn
    return jnp.concatenate([turned, grads_part[..., ROT:]], axis=-1)


def build_mask(segment_rows):
    places = jnp.arange(segment_rows.shape[-1], dtype=jnp.int32)
    return (segment_rows[:, :, None] == segment_rows[:, None, :]) & (
        places[None, :] <= places[:, None]
    )


def attention_scores(queries, keys_rot):
    return (
        jnp.einsum("bqhd,bkhd->bhqk", queries, keys_rot, preferred_element_type=jnp.float32) * SCALE
    )


def attend_forward(queries, keys_rot, values, mask):
    scores = jnp.where(mask[:, None], attention_scores(queries, keys_rot), NEGATIVE)
    row_top = jnp.max(scores, axis=-1, keepdims=True)
    exponent = jnp.exp(scores - row_top)
    row_total = jnp.sum(exponent, axis=-1, keepdims=True)
    attention = (exponent / row_total).astype(jnp.bfloat16)
    context = jnp.einsum("bhqk,bkhd->bqhd", attention, values, preferred_element_type=jnp.float32)
    return (context.astype(jnp.bfloat16), row_top + jnp.log(row_total))


def attend_backward(queries, keys_rot, values, mask, log_total, context_grad):
    scores = attention_scores(queries, keys_rot)
    attention = jnp.where(mask[:, None], jnp.exp(scores - log_total), 0.0)
    value_grad = jnp.einsum(
        "bhqk,bqhd->bkhd",
        attention.astype(jnp.bfloat16),
        context_grad,
        preferred_element_type=jnp.float32,
    )
    attention_grad = jnp.einsum(
        "bqhd,bkhd->bhqk", context_grad, values, preferred_element_type=jnp.float32
    )
    row_centre = jnp.sum(attention * attention_grad, axis=-1, keepdims=True)
    score_grad = (attention * (attention_grad - row_centre)).astype(jnp.bfloat16)
    query_grad = (
        jnp.einsum("bhqk,bkhd->bqhd", score_grad, keys_rot, preferred_element_type=jnp.float32)
        * SCALE
    )
    key_grad = (
        jnp.einsum("bhqk,bqhd->bkhd", score_grad, queries, preferred_element_type=jnp.float32)
        * SCALE
    )
    return (query_grad, key_grad, value_grad)


def sum_over_line(partial):
    inward = lax.ppermute(partial, "sp", [(0, 1), (3, 2)])
    half = rounded(partial.astype(jnp.float32) + inward.astype(jnp.float32))
    other = lax.ppermute(half, "sp", [(1, 2), (2, 1)])
    whole = rounded(half.astype(jnp.float32) + other.astype(jnp.float32))
    outward = lax.ppermute(whole, "sp", [(1, 0), (2, 3)])
    place = lax.axis_index("sp")
    inner = (place == 1) | (place == 2)
    return jnp.where(inner, whole, outward).astype(jnp.float32)


def sum_over_sp(partial):
    partial = rounded(partial)
    if lax.axis_size("sp") == 4:
        return sum_over_line(partial)
    return lax.psum(partial, "sp").astype(jnp.float32)


def per_device(
    hidden_in,
    segments,
    ln1_gain,
    ln1_bias,
    ln2_gain,
    ln2_bias,
    w_qkv,
    b_qkv,
    w_dense,
    b_dense,
    w_up,
    b_up,
    w_down,
    b_down,
    cotangent,
):
    seq_local, shard_len, width = hidden_in.shape
    seq_len = segments.shape[1]
    nf, ns = (lax.axis_size("fsdp"), lax.axis_size("sp"))
    f_place, s_place = (lax.axis_index("fsdp"), lax.axis_index("sp"))
    seqs = seq_local * nf
    group = seqs // ns
    piece = shard_len // nf
    tokens = group * seq_len
    per_head = max(1, nf // HEADS)
    head_count = max(1, HEADS // nf)
    head_sets = [[head * per_head + k for k in range(per_head)] for head in range(nf // per_head)]

    def gather_tokens(block):
        part = lax.all_to_all(block, "fsdp", split_axis=1, concat_axis=0, tiled=True)
        part = lax.all_to_all(part, "sp", split_axis=0, concat_axis=1, tiled=True)
        return lax.all_gather(part, "fsdp", axis=0, tiled=True).reshape(tokens, width)

    def scatter_tokens(partial):
        part = partial.reshape(nf * group, ns * piece, width)
        part = lax.psum_scatter(part, "fsdp", scatter_dimension=0, tiled=True)
        part = lax.all_to_all(part, "sp", split_axis=1, concat_axis=0, tiled=True)
        return lax.all_to_all(part, "fsdp", split_axis=0, concat_axis=1, tiled=True)

    def in_order(array):
        array = array.reshape(nf, group, ns, piece, -1)
        return array.transpose(1, 2, 0, 3, 4).reshape(group, seq_len, -1)

    def out_of_order(array):
        array = array.reshape(group, ns, nf, piece, -1)
        return array.transpose(2, 0, 1, 3, 4).reshape(tokens, -1)

    def over_head(array, axis):
        if per_head == 1:
            return array
        return lax.all_gather(array, "fsdp", axis=axis, tiled=True, axis_index_groups=head_sets)

    def own_columns(array):
        if per_head == 1:
            return array
        share = array.shape[-1] // per_head
        return lax.dynamic_slice_in_dim(array, f_place % per_head * share, share, array.ndim - 1)

    def own_part(vector):
        share = vector.shape[0] // nf
        return lax.dynamic_slice_in_dim(vector, f_place * share, share, 0)

    gathered = gather_tokens(hidden_in)
    upstream = gather_tokens(cotangent)
    rows = lax.all_gather(segments, "fsdp", axis=0, tiled=True)
    rows = lax.dynamic_slice_in_dim(rows, s_place * group, group, 0)
    dense_in = lax.all_to_all(w_dense, "fsdp", split_axis=1, concat_axis=0, tiled=True)
    head_qkv = over_head(w_qkv, 0)
    head_dense = over_head(dense_in, 1)
    head_bias = lax.dynamic_slice_in_dim(
        b_qkv, f_place // per_head * head_qkv.shape[0], head_qkv.shape[0], 0
    )
    scaled, _ = norm_scaled(gathered.astype(jnp.float32))
    normed = (scaled * ln1_gain + ln1_bias).astype(jnp.bfloat16)
    normed_mlp = (scaled * ln2_gain + ln2_bias).astype(jnp.bfloat16)
    hidden = times_transposed(normed_mlp, w_up) + own_part(b_up)
    activated, slope = gelu_pair(hidden)
    activated = activated.astype(jnp.bfloat16)
    hidden_grad = (times_transposed(upstream, w_down) * slope).astype(jnp.bfloat16)
    down_term = contract_rows(activated, upstream)
    up_term = contract_rows(hidden_grad, normed_mlp)
    mlp_norm_grad = times(hidden_grad, w_up)
    packed = (times_transposed(normed, head_qkv) + head_bias).astype(jnp.bfloat16)
    packed = in_order(packed).reshape(group, seq_len, head_count, 3 * HEAD_DIM)
    cos_table, sin_table = rotary_tables(rows)
    queries = rotate(packed[..., :HEAD_DIM].astype(jnp.float32), cos_table, sin_table).astype(
        jnp.bfloat16
    )
    keys_rot = rotate(
        packed[..., HEAD_DIM : 2 * HEAD_DIM].astype(jnp.float32), cos_table, sin_table
    ).astype(jnp.bfloat16)
    values = packed[..., 2 * HEAD_DIM :]
    mask = build_mask(rows)
    context, log_total = attend_forward(queries, keys_rot, values, mask)
    context = own_columns(out_of_order(context))
    partial_out = times_transposed(context, dense_in) + times(activated, w_down)
    context_grad = in_order(times(upstream, head_dense).astype(jnp.bfloat16)).reshape(
        group, seq_len, head_count, HEAD_DIM
    )
    query_grad, key_grad, value_grad = attend_backward(
        queries, keys_rot, values, mask, log_total, context_grad
    )
    packed_grad = jnp.concatenate(
        [
            unrotate(query_grad, cos_table, sin_table),
            unrotate(key_grad, cos_table, sin_table),
            value_grad,
        ],
        axis=-1,
    ).astype(jnp.bfloat16)
    packed_grad = own_columns(out_of_order(packed_grad))
    attn_norm_grad = times(packed_grad, w_qkv)
    qkv_term = contract_rows(packed_grad, normed)
    dense_term = contract_rows(upstream, context).astype(jnp.bfloat16)
    dense_term = lax.all_to_all(dense_term, "fsdp", split_axis=0, concat_axis=1, tiled=True)
    vectors = jnp.stack(
        [
            jnp.sum(attn_norm_grad * scaled, axis=0),
            jnp.sum(attn_norm_grad, axis=0),
            jnp.sum(mlp_norm_grad * scaled, axis=0),
            jnp.sum(mlp_norm_grad, axis=0),
        ],
        axis=1,
    )
    vectors = lax.psum_scatter(vectors, "fsdp", scatter_dimension=0, tiled=True)
    bias_out = own_part(jnp.sum(upstream.astype(jnp.float32), axis=0))
    bias_qkv = jnp.sum(packed_grad.astype(jnp.float32), axis=0)
    bias_up = jnp.sum(hidden_grad.astype(jnp.float32), axis=0)
    vectors, bias_out, bias_qkv, bias_up = lax.psum((vectors, bias_out, bias_qkv, bias_up), "sp")
    output = scatter_tokens(rounded(partial_out))
    weighted = scatter_tokens(rounded(attn_norm_grad * ln1_gain + mlp_norm_grad * ln2_gain))
    inputs = hidden_in.astype(jnp.float32)
    output = (inputs + (output.astype(jnp.float32) + (b_dense + b_down))).astype(jnp.bfloat16)
    own_scaled, own_inverse = norm_scaled(inputs)
    weighted = weighted.astype(jnp.float32)
    first_mean = jnp.mean(weighted, axis=-1, keepdims=True)
    second_mean = jnp.mean(weighted * own_scaled, axis=-1, keepdims=True)
    input_grad = (
        cotangent.astype(jnp.float32)
        + own_inverse * (weighted - first_mean - own_scaled * second_mean)
    ).astype(jnp.bfloat16)
    grad_down_w = sum_over_sp(down_term)
    grad_up_w = sum_over_sp(up_term)
    grad_qkv_w = sum_over_sp(qkv_term)
    grad_dense_w = sum_over_sp(dense_term)
    return (
        output,
        input_grad,
        vectors[:, 0],
        vectors[:, 1],
        vectors[:, 2],
        vectors[:, 3],
        grad_qkv_w,
        bias_qkv,
        grad_dense_w,
        bias_out,
        grad_up_w,
        bias_up,
        grad_down_w,
        bias_out,
    )


def solution(mesh):
    rows = P("fsdp", "sp", None)
    first = P("fsdp", None)
    return jax.shard_map(
        per_device,
        mesh=mesh,
        in_specs=(
            rows,
            first,
            P(),
            P(),
            P(),
            P(),
            first,
            P(),
            first,
            P(),
            first,
            P(),
            first,
            P(),
            rows,
        ),
        out_specs=(
            rows,
            rows,
            P("fsdp"),
            P("fsdp"),
            P("fsdp"),
            P("fsdp"),
            first,
            P("fsdp"),
            first,
            P("fsdp"),
            first,
            P("fsdp"),
            first,
            P("fsdp"),
        ),
        check_vma=False,
    )
```

profile of v0, /device:TPU:0, one launch (start us, length us, event | category | flops | bytes accessed | tf_op | source)
XLA Modules:
  0.0 1062.1 jit_solution(14219116837195556078)
XLA Ops:
  7.2 4.3 copy.236
  12.1 9.0 reduce.19
  23.7 20.6 %all_to_all.146 = bf16[8,2,32768]{2,1,0:T(2,128)(2,1)} all-to-all(bf16[8,2,32768]{2,1,0:T(2,128)(2,1)} %reshape.579), channel_id=1, replica_groups=mesh['fsdp'=8,'sp'=4] {'fsdp'}, dimensions={0} | all-to-all | bytes 2097152 | tf_op jit(solution)/shard_map/all_to_all | solution.py:185
  44.3 5.8 reshape.580
  52.3 30.2 %all_to_all.147 = bf16[8,32,2048]{2,1,0:T(8,128)(2,1)S(1)} all-to-all(bf16[8,32,2048]{2,1,0:T(8,128)(2,1)S(1)} %bitcast.199), channel_id=1, replica_groups=mesh['fsdp'=8,'sp'=4] {'sp'}, dimensions={0} | all-to-all | bytes 2097152 | tf_op jit(solution)/shard_map/all_to_all | solution.py:186
  83.8 4.2 copy.235
  88.0 9.2 reduce.20
  99.8 26.8 %all_to_all.148 = bf16[8,2,32768]{2,1,0:T(2,128)(2,1)} all-to-all(bf16[8,2,32768]{2,1,0:T(2,128)(2,1)} %reshape.581), channel_id=1, replica_groups=mesh['fsdp'=8,'sp'=4] {'fsdp'}, dimensions={0} | all-to-all | bytes 2097152 | tf_op jit(solution)/shard_map/all_to_all | solution.py:185
  126.6 5.8 reshape.582
  134.6 26.5 %all_to_all.149 = bf16[8,32,2048]{2,1,0:T(8,128)(2,1)S(1)} all-to-all(bf16[8,32,2048]{2,1,0:T(8,128)(2,1)S(1)} %bitcast.200), channel_id=1, replica_groups=mesh['fsdp'=8,'sp'=4] {'sp'}, dimensions={0} | all-to-all | bytes 2097152 | tf_op jit(solution)/shard_map/all_to_all | solution.py:186
  164.4 4.3 all-to-all-start.2
  168.7 26.7 %all-gather = s32[8,1,1024]{2,1,0:T(1,128)S(1)} all-gather(s32[1,1,1024]{2,1,0:T(1,128)S(1)} %bitcast.233), channel_id=1, replica_groups=mesh['fsdp'=8,'sp'=4] {'fsdp'}, dimensions={0}, use_global_device_ids=true | all-gather | bytes 36864 | tf_op jit(solution)/shard_map/all_gather | solution.py:220
  203.1 4.7 convert_reduce_fusion.1
  212.1 7.4 add_convert_fusion.2
  219.4 7.1 add_convert_fusion.3
  231.5 6.1 convolution_convert_fusion.1
  238.8 4.9 fusion.41
  247.0 3.3 fusion.8
  250.4 4.7 fusion.28
  255.1 5.1 multiply_reduce_fusion.3
  260.1 3.7 multiply_convert_fusion
  271.8 4.6 slice_multiply_fusion.2
  282.8 5.0 fusion.37
  287.8 7.0 concatenate.117
  294.8 3.9 copy.201
  298.7 15.7 %multiply_convert_fusion.1 = (bf16[2048,1024]{1,0:T(8,128)(2,1)}, f32[2048,1024]{1,0:T(8,128)}) fusion(f32[1024]{0:T(1024)S(1)} %dynamic_slice.14, bf16[2048,2048]{1,0:T(8,128)(2,1)} %get-tuple-element.26, bf16[1024,2048]{1,0:T(8,128)(2,1)S(1)} %copy-done.39), kind=kOutput, calls=%fused_computation.29 | convolution fusion | flops 8602517504 | bytes 25169920 | tf_op jit(solution)/shard_map/dot_general | solution.py:28
  314.4 17.5 %convert_reduce_fusion.2 = (f32[1024]{0:T(1024)}, bf16[2048,1024]{1,0:T(8,128)(2,1)}) fusion(f32[2048,1024]{1,0:T(8,128)} %get-tuple-element.60, f32[1024]{0:T(1024)S(1)} %dynamic_slice.14, bf16[2048,2048]{1,0:T(8,128)(2,1)S(1)} %bitcast.176, bf16[1024,2048]{1,0:T(8,128)(2,1)} %param.27), kind=kOutput, calls=%fused_computation.22 | convolution fusion | flops 8617196544 | bytes 25174016 | tf_op jit(solution)/shard_map/dot_general | solution.py:28
  331.9 14.1 %fusion.59 = f32[2048,2048]{1,0:T(8,128)} fusion(bf16[2048,1024]{1,0:T(8,128)(2,1)} %get-tuple-element.62, bf16[1024,2048]{1,0:T(8,128)(2,1)S(1)} %copy-done.39), kind=kOutput, calls=%fused_computation.148 | convolution fusion | flops 8589934592 | bytes 25165824 | tf_op jit(solution)/shard_map/dot_general | solution.py:34
  346.0 17.8 %multiply_reduce_fusion.1 = (f32[2048]{0:T(1024)S(1)}, f32[2048]{0:T(1024)S(1)}, f32[2048]{0:T(1024)S(1)}, f32[2048]{0:T(1024)S(1)}, bf16[2048,2048]{1,0:T(8,128)(2,1)}) fusion(bf16[16,128,2048]{2,1,0:T(8,128)(2,1)} %all-gather.4.cloned.1.call-done, f32[2048]{0:T(1024)S(1)} %get-tuple-element.48, f32[2048]{0:T(1024)S(1)} %get-tuple-element.49, ...), kind=kOutput, calls=%fused_computation.5 | convolution fusion | flops 6501163008 | bytes 39911424 | tf_op jit(solution)/shard_map/dot_general | solution.py:34
  365.0 7.5 fusion.31
  373.6 15.8 %reduce-precision_convert_fusion.7 = bf16[1024,2048]{1,0:T(8,128)(2,1)} fusion(bf16[2048,1024]{1,0:T(8,128)(2,1)} %get-tuple-element.62, bf16[2048,2048]{1,0:T(8,128)(2,1)} %get-tuple-element.26), kind=kOutput, calls=%fused_computation.25 | convolution fusion | flops 8594128896 | bytes 16777216 | tf_op jit(solution)/shard_map/dot_general | solution.py:22
  389.4 5.6 collective-permute-start.6
  395.1 11.7 %fusion.58 = f32[2048,2048]{1,0:T(8,128)} fusion(bf16[2048,1024]{1,0:T(8,128)(2,1)S(1)} %copy-done.41, bf16[1024,2048]{1,0:T(8,128)(2,1)S(1)} %copy-done.40), kind=kOutput, calls=%fused_computation.147 | convolution fusion | flops 8589934592 | bytes 25165824 | tf_op jit(solution)/shard_map/dot_general | solution.py:34
  406.8 11.7 %reduce-precision_convert_fusion.1 = bf16[2048,2048]{1,0:T(8,128)(2,1)} fusion(f32[2048,2048]{1,0:T(8,128)} %fusion.58, bf16[2048,256]{1,0:T(8,128)(2,1)S(1)} %bitcast.188, bf16[2048,256]{1,0:T(8,128)(2,1)S(1)} %bitcast.212), kind=kOutput, calls=%fused_computation.7 | convolution fusion | flops 2160066560 | bytes 27262976 | tf_op jit(solution)/shard_map/dot_general | solution.py:28
  418.5 14.7 %reduce-precision_convert_fusion.4 = bf16[1024,2048]{1,0:T(8,128)(2,1)} fusion(bf16[2048,1024]{1,0:T(8,128)(2,1)} %get-tuple-element.59, bf16[2048,2048]{1,0:T(8,128)(2,1)} %bitcast.173), kind=kOutput, calls=%fused_computation.21 | convolution fusion | flops 8594128896 | bytes 16777216 | tf_op jit(solution)/shard_map/dot_general | solution.py:22
  433.2 3.3 collective-permute-start.9
  436.5 6.3 add_convert_fusion
  442.8 8.3 reduce-precision_convert_fusion.10
  454.0 30.2 %collective-permute-done.6 = bf16[1024,2048]{1,0:T(8,128)(2,1)} collective-permute-done((bf16[1024,2048]{1,0:T(8,128)(2,1)}, bf16[1024,2048]{1,0:T(8,128)(2,1)}, u32[]{:S(2)}, u32[]{:S(2)}) %collective-permute-start.6) | collective-permute-done | bytes 4194336 | tf_op jit(solution)/shard_map/ppermute | solution.py:138
  484.3 7.9 reduce-precision_convert_fusion.6
  498.2 3.6 all-to-all-start.9
  501.8 72.4 %collective-permute-done.9 = bf16[1024,2048]{1,0:T(8,128)(2,1)} collective-permute-done((bf16[1024,2048]{1,0:T(8,128)(2,1)}, bf16[1024,2048]{1,0:T(8,128)(2,1)}, u32[]{:S(2)}, u32[]{:S(2)}) %collective-permute-start.9) | collective-permute-done | bytes 4194336 | tf_op jit(solution)/shard_map/ppermute | solution.py:138
  574.1 7.7 reduce-precision_convert_fusion.3
  584.6 56.3 %collective-permute-done = bf16[768,2048]{1,0:T(8,128)(2,1)} collective-permute-done((bf16[768,2048]{1,0:T(8,128)(2,1)}, bf16[768,2048]{1,0:T(8,128)(2,1)}, u32[]{:S(2)}, u32[]{:S(2)}) %collective-permute-start) | collective-permute-done | bytes 3145760 | tf_op jit(solution)/shard_map/ppermute | solution.py:138
  640.9 6.1 reduce-precision_convert_fusion.9
  650.1 4.9 collective-permute-start.3
  655.6 20.9 %collective-permute-done.3 = bf16[256,2048]{1,0:T(8,128)(2,1)S(1)} collective-permute-done((bf16[256,2048]{1,0:T(8,128)(2,1)S(1)}, bf16[256,2048]{1,0:T(8,128)(2,1)S(1)}, u32[]{:S(2)}, u32[]{:S(2)}) %collective-permute-start.3) | collective-permute-done | bytes 1048608 | tf_op jit(solution)/shard_map/ppermute | solution.py:138
  677.6 7.7 reduce-precision_convert_fusion.5
  686.6 6.1 reduce-precision_convert_fusion.8
  694.0 3.3 copy.202
  697.3 63.8 %all-to-all-start.7 = ((bf16[2,128,2048]{2,0,1:T(2,128)(2,1)}), bf16[2,128,2048]{2,0,1:T(2,128)(2,1)}, u32[]{:S(2)}, u32[]{:S(2)}) async-start(bf16[2,128,2048]{2,0,1:T(2,128)(2,1)} %copy.202), calls=%async_computation.9 | async-start | bytes 2097152 | tf_op jit(solution)/shard_map/all_to_all | solution.py:192
  761.2 7.7 reduce-precision_convert_fusion.2
  774.3 3.4 copy.186
  777.8 89.9 %all-to-all-done.7 = bf16[2,128,2048]{2,0,1:T(2,128)(2,1)} async-done(((bf16[2,128,2048]{2,0,1:T(2,128)(2,1)}), bf16[2,128,2048]{2,0,1:T(2,128)(2,1)}, u32[]{:S(2)}, u32[]{:S(2)}) %all-to-all-start.7) | async-done | bytes 1048608 | tf_op jit(solution)/shard_map/all_to_all | solution.py:192
  867.7 4.5 all-to-all-start.3
  872.2 4.7 convert_reduce_fusion
  878.6 126.6 %all-reduce.1 = (f32[256,4]{0,1:T(4,128)S(1)}, f32[768]{0:T(1024)}, f32[256]{0:T(256)S(1)}, f32[1024]{0:T(1024)}) all-reduce(f32[256,4]{0,1:T(4,128)S(1)} %copy.219, f32[768]{0:T(1024)S(1)} %convert_reduce_fusion.3, f32[256]{0:T(256)S(1)} %dynamic_slice.15, f32[1024]{0:T(1024)S(1)} %copy-done.37), channel_id=1, replica_groups=mesh['fsdp'=8,'sp'=4] {'sp'}, use_global_device_ids=true, to_apply=%region_18.19 | all-reduce | flops 3072 | bytes 24576 | tf_op jit(solution)/shard_map/psum | solution.py:284
  1011.2 3.6 all-to-all-start.8
  1014.7 5.0 select_convert_fusion.2
  1019.8 6.1 select_convert_fusion.1
  1030.1 4.2 all-to-all-start.4
  1034.3 6.1 select_convert_fusion
  1045.5 4.2 all-to-all-done.4
  1049.7 4.9 fusion.21
  (202 shorter events, 94.4 us)
Async XLA Ops:
  7.2 212.3 %copy-start = (bf16[768,2048]{1,0:T(8,128)(2,1)S(1)}, bf16[768,2048]{1,0:T(8,128)(2,1)}, u32[]{:S(2)}) copy-start(bf16[768,2048]{1,0:T(8,128)(2,1)} %param.21) | copy-start | bytes 9437188
  7.2 195.9 %all-gather.4.cloned.1.call-start = ((), (), s32[]{:S(2)}) async-start(), calls=%async_computation.13 | async-start | bytes 9437184 | tf_op jit(solution)/shard_map/all_gather | solution.py:187
  83.5 147.9 %all-gather.6.cloned.1.call-start = ((), (), s32[]{:S(2)}) async-start(), calls=%async_computation.15 | async-start | bytes 9437184 | tf_op jit(solution)/shard_map/all_gather | solution.py:187
  132.3 36.4 %copy-start.36 = (s32[1,1024]{1,0:T(1,128)S(1)}, s32[1,1024]{1,0:T(1,128)}, u32[]{:S(2)}) copy-start(s32[1,1024]{1,0:T(1,128)} %param.16) | copy-start | bytes 12292
  164.4 36.5 %all-to-all-start.2 = ((bf16[256,8,256]{0,2,1:T(8,128)(2,1)}), bf16[256,8,256]{0,2,1:T(8,128)(2,1)}, u32[]{:S(2)}, u32[]{:S(2)}) async-start(bf16[256,8,256]{0,2,1:T(8,128)(2,1)} %bitcast.204), calls=%async_computation.2 | async-start | bytes 2097152 | tf_op jit(solution)/shard_map/all_to_all | solution.py:222
  168.7 525.4 %reduce-scatter.8.cloned.1.call-start = ((), (), s32[]{:S(2)}) async-start(), calls=%async_computation.16 | async-start | bytes 9437184 | tf_op jit(solution)/shard_map/reduce_scatter | solution.py:191
  203.1 5.9 copy-start.2
  207.9 4.2 copy-start.28
  207.9 4.2 copy-start.30
  207.9 4.2 copy-start.32
  207.9 4.2 copy-start.33
  207.9 11.5 %copy-start.26 = (f32[16,128]{1,0:T(8,128)}, f32[16,128]{1,0:T(8,128)S(1)}, u32[]{:S(2)}) copy-start(f32[16,128]{1,0:T(8,128)S(1)} %get-tuple-element.50) | copy-start | bytes 24580
  231.5 6.2 copy-start.12
  231.5 6.2 copy-start.13
  238.4 5.3 copy-start.15
  238.4 5.3 copy-start.19
  238.4 5.3 copy-start.24
  243.7 3.2 copy-start.22
  243.7 3.2 copy-start.25
  247.0 13.2 %copy-start.3 = (f32[2,1024,1024]{1,2,0:T(8,128)}, f32[2,1024,1024]{1,2,0:T(8,128)S(1)}, u32[]{:S(2)}) copy-start(f32[2,1024,1024]{1,2,0:T(8,128)S(1)} %get-tuple-element.56) | copy-start | bytes 25165828
  266.7 5.1 copy-start.17
  268.8 3.0 copy-start.10
  278.7 4.1 copy-start.9
  278.7 4.1 copy-start.11
  278.7 4.1 copy-start.18
  294.8 3.9 copy-start.39
  294.8 19.6 %slice-start = ((s8[8388608]{0:T(1024)(128)(4,1)}), s8[4194304]{0:T(1024)(128)(4,1)S(1)}, s32[]{:S(2)}) async-start(s8[8388608]{0:T(1024)(128)(4,1)} %bitcast.174), calls=%async_computation.18 | async-start | bytes 8388608
  298.7 15.7 %slice-start.1 = ((s8[8388608]{0:T(1024)(128)(4,1)}), s8[4194304]{0:T(1024)(128)(4,1)S(1)}, s32[]{:S(2)}) async-start(s8[8388608]{0:T(1024)(128)(4,1)} %bitcast.174), calls=%async_computation.19 | async-start | bytes 8388608
  363.8 410.5 %reduce-scatter.6.cloned.1.call-start = ((), (), s32[]{:S(2)}) async-start(), calls=%async_computation.14 | async-start | bytes 9437184 | tf_op jit(solution)/shard_map/reduce_scatter | solution.py:191
  373.6 21.4 %copy-start.40 = (bf16[1024,2048]{1,0:T(8,128)(2,1)S(1)}, bf16[1024,2048]{1,0:T(8,128)(2,1)}, u32[]{:S(2)}) copy-start(bf16[1024,2048]{1,0:T(8,128)(2,1)} %param.27) | copy-start | bytes 12582916
  373.6 21.4 %copy-start.41 = (bf16[2048,1024]{1,0:T(8,128)(2,1)S(1)}, bf16[2048,1024]{1,0:T(8,128)(2,1)}, u32[]{:S(2)}) copy-start(bf16[2048,1024]{1,0:T(8,128)(2,1)} %get-tuple-element.59) | copy-start | bytes 12582916
  389.4 94.8 %collective-permute-start.6 = (bf16[1024,2048]{1,0:T(8,128)(2,1)}, bf16[1024,2048]{1,0:T(8,128)(2,1)}, u32[]{:S(2)}, u32[]{:S(2)}) collective-permute-start(bf16[1024,2048]{1,0:T(8,128)(2,1)} %reduce-precision_convert_fusion.7), channel_id=1, source_target_pairs={{0,1},{3,2},{4,5},{7,6},{8,9},{11,10},{12,13},{15,14},{16,17},{19,... | collective-permute-start | bytes 12582920 | tf_op jit(solution)/shard_map/ppermute | solution.py:138
  395.1 11.7 %copy-start.20 = (bf16[8,256,256]{2,1,0:T(8,128)(2,1)S(1)}, bf16[8,256,256]{2,1,0:T(8,128)(2,1)}, u32[]{:S(2)}) copy-start(bf16[8,256,256]{2,1,0:T(8,128)(2,1)} %copy.185) | copy-start | bytes 3145732
  418.4 18.0 %copy-start.27 = (f32[16,128]{1,0:T(8,128)S(1)}, f32[16,128]{1,0:T(8,128)}, u32[]{:S(2)}) copy-start(f32[16,128]{1,0:T(8,128)} %copy-done.26) | copy-start | bytes 24580
  418.4 18.0 %copy-start.29 = (f32[2048]{0:T(1024)S(1)}, f32[2048]{0:T(1024)}, u32[]{:S(2)}) copy-start(f32[2048]{0:T(1024)} %param.18) | copy-start | bytes 24580
  418.5 18.0 %copy-start.31 = (f32[16,128]{1,0:T(8,128)S(1)}, f32[16,128]{1,0:T(8,128)}, u32[]{:S(2)}) copy-start(f32[16,128]{1,0:T(8,128)} %get-tuple-element.47) | copy-start | bytes 24580
  433.2 140.9 %collective-permute-start.9 = (bf16[1024,2048]{1,0:T(8,128)(2,1)}, bf16[1024,2048]{1,0:T(8,128)(2,1)}, u32[]{:S(2)}, u32[]{:S(2)}) collective-permute-start(bf16[1024,2048]{1,0:T(8,128)(2,1)} %reduce-precision_convert_fusion.4), channel_id=1, source_target_pairs={{0,1},{3,2},{4,5},{7,6},{8,9},{11,10},{12,13},{15,14},{16,17},{19,... | collective-permute-start | bytes 12582920 | tf_op jit(solution)/shard_map/ppermute | solution.py:138
  436.5 6.3 copy-start.21
  442.7 52.1 %slice-start.2 = ((s8[8388608]{0:T(1024)(128)(4,1)}), s8[4194304]{0:T(1024)(128)(4,1)S(1)}, s32[]{:S(2)}) async-start(s8[8388608]{0:T(1024)(128)(4,1)} %bitcast.177), calls=%async_computation.20 | async-start | bytes 8388608
  442.8 52.1 %slice-start.3 = ((s8[8388608]{0:T(1024)(128)(4,1)}), s8[4194304]{0:T(1024)(128)(4,1)S(1)}, s32[]{:S(2)}) async-start(s8[8388608]{0:T(1024)(128)(4,1)} %bitcast.177), calls=%async_computation.21 | async-start | bytes 8388608
  451.1 189.8 %collective-permute-start = (bf16[768,2048]{1,0:T(8,128)(2,1)}, bf16[768,2048]{1,0:T(8,128)(2,1)}, u32[]{:S(2)}, u32[]{:S(2)}) collective-permute-start(bf16[768,2048]{1,0:T(8,128)(2,1)} %reduce-precision_convert_fusion.10), channel_id=1, source_target_pairs={{0,1},{3,2},{4,5},{7,6},{8,9},{11,10},{12,13},{15,14},{16,17},{19,... | collective-permute-start | bytes 9437192 | tf_op jit(solution)/shard_map/ppermute | solution.py:138
  492.1 185.5 %collective-permute-start.7 = (bf16[1024,2048]{1,0:T(8,128)(2,1)}, bf16[1024,2048]{1,0:T(8,128)(2,1)}, u32[]{:S(2)}, u32[]{:S(2)}) collective-permute-start(bf16[1024,2048]{1,0:T(8,128)(2,1)} %reduce-precision_convert_fusion.6), channel_id=1, source_target_pairs={{1,2},{2,1},{5,6},{6,5},{9,10},{10,9},{13,14},{14,13},{17,18},{18,... | collective-permute-start | bytes 12582920 | tf_op jit(solution)/shard_map/ppermute | solution.py:140
  498.2 151.1 %all-to-all-start.9 = ((bf16[8,256,256]{1,2,0:T(8,128)(2,1)}), bf16[8,256,256]{1,2,0:T(8,128)(2,1)S(1)}, u32[]{:S(2)}, u32[]{:S(2)}) async-start(bf16[8,256,256]{1,2,0:T(8,128)(2,1)} %bitcast.164), calls=%async_computation.11 | async-start | bytes 2097152 | tf_op jit(solution)/shard_map/all_to_all | solution.py:270
  581.8 73.1 %copy-start.5 = (bf16[1,256,2048]{2,1,0:T(8,128)(2,1)S(1)}, bf16[1,256,2048]{2,1,0:T(8,128)(2,1)}, u32[]{:S(2)}) copy-start(bf16[1,256,2048]{2,1,0:T(8,128)(2,1)} %param.15) | copy-start | bytes 3145732
  581.8 179.4 %collective-permute-start.10 = (bf16[1024,2048]{1,0:T(8,128)(2,1)}, bf16[1024,2048]{1,0:T(8,128)(2,1)}, u32[]{:S(2)}, u32[]{:S(2)}) collective-permute-start(bf16[1024,2048]{1,0:T(8,128)(2,1)} %reduce-precision_convert_fusion.3), channel_id=1, source_target_pairs={{1,2},{2,1},{5,6},{6,5},{9,10},{10,9},{13,14},{14,13},{17,18},{18,... | collective-permute-start | bytes 12582920 | tf_op jit(solution)/shard_map/ppermute | solution.py:140
  647.0 39.6 %collective-permute-start.1 = (bf16[768,2048]{1,0:T(8,128)(2,1)}, bf16[768,2048]{1,0:T(8,128)(2,1)}, u32[]{:S(2)}, u32[]{:S(2)}) collective-permute-start(bf16[768,2048]{1,0:T(8,128)(2,1)} %reduce-precision_convert_fusion.9), channel_id=1, source_target_pairs={{1,2},{2,1},{5,6},{6,5},{9,10},{10,9},{13,14},{14,13},{17,18},{18,... | collective-permute-start | bytes 9437192 | tf_op jit(solution)/shard_map/ppermute | solution.py:140
  650.1 26.4 %collective-permute-start.3 = (bf16[256,2048]{1,0:T(8,128)(2,1)S(1)}, bf16[256,2048]{1,0:T(8,128)(2,1)S(1)}, u32[]{:S(2)}, u32[]{:S(2)}) collective-permute-start(bf16[256,2048]{1,0:T(8,128)(2,1)S(1)} %copy.206), channel_id=1, source_target_pairs={{0,1},{3,2},{4,5},{7,6},{8,9},{11,10},{12,13},{15,14},{16,17},{19,... | collective-permute-start | bytes 3145736 | tf_op jit(solution)/shard_map/ppermute | solution.py:138
  676.9 93.4 %collective-permute-start.4 = (bf16[256,2048]{1,0:T(8,128)(2,1)S(1)}, bf16[256,2048]{1,0:T(8,128)(2,1)S(1)}, u32[]{:S(2)}, u32[]{:S(2)}) collective-permute-start(bf16[256,2048]{1,0:T(8,128)(2,1)S(1)} %reduce-precision_convert_fusion.12), channel_id=1, source_target_pairs={{1,2},{2,1},{5,6},{6,5},{9,10},{10,9},{13,14},{14,13},{17,18},{18,... | collective-permute-start | bytes 3145736 | tf_op jit(solution)/shard_map/ppermute | solution.py:140
  685.3 334.4 %collective-permute-start.8 = (bf16[1024,2048]{1,0:T(8,128)(2,1)}, bf16[1024,2048]{1,0:T(8,128)(2,1)}, u32[]{:S(2)}, u32[]{:S(2)}) collective-permute-start(bf16[1024,2048]{1,0:T(8,128)(2,1)} %reduce-precision_convert_fusion.5), channel_id=1, source_target_pairs={{1,0},{2,3},{5,4},{6,7},{9,8},{10,11},{13,12},{14,15},{17,16},{18,... | collective-permute-start | bytes 12582920 | tf_op jit(solution)/shard_map/ppermute | solution.py:142
  692.7 322.0 %collective-permute-start.2 = (bf16[768,2048]{1,0:T(8,128)(2,1)}, bf16[768,2048]{1,0:T(8,128)(2,1)}, u32[]{:S(2)}, u32[]{:S(2)}) collective-permute-start(bf16[768,2048]{1,0:T(8,128)(2,1)} %reduce-precision_convert_fusion.8), channel_id=1, source_target_pairs={{1,0},{2,3},{5,4},{6,7},{9,8},{10,11},{13,12},{14,15},{17,16},{18,... | collective-permute-start | bytes 9437192 | tf_op jit(solution)/shard_map/ppermute | solution.py:142
  697.3 170.4 %all-to-all-start.7 = ((bf16[2,128,2048]{2,0,1:T(2,128)(2,1)}), bf16[2,128,2048]{2,0,1:T(2,128)(2,1)}, u32[]{:S(2)}, u32[]{:S(2)}) async-start(bf16[2,128,2048]{2,0,1:T(2,128)(2,1)} %copy.202), calls=%async_computation.9 | async-start | bytes 2097152 | tf_op jit(solution)/shard_map/all_to_all | solution.py:192
  761.1 9.0 copy-start.34
  761.1 9.1 copy-start.35
  761.1 116.5 %reduce-scatter.10.cloned.1.call-start = ((), (), s32[]{:S(2)}) async-start(), calls=%async_computation.17 | async-start | bytes 1179648
  768.9 265.4 %collective-permute-start.11 = (bf16[1024,2048]{1,0:T(8,128)(2,1)}, bf16[1024,2048]{1,0:T(8,128)(2,1)}, u32[]{:S(2)}, u32[]{:S(2)}) collective-permute-start(bf16[1024,2048]{1,0:T(8,128)(2,1)} %reduce-precision_convert_fusion.2), channel_id=1, source_target_pairs={{1,0},{2,3},{5,4},{6,7},{9,8},{10,11},{13,12},{14,15},{17,16},{18,... | collective-permute-start | bytes 12582920 | tf_op jit(solution)/shard_map/ppermute | solution.py:142
  771.6 234.2 %collective-permute-start.5 = (bf16[256,2048]{1,0:T(8,128)(2,1)}, bf16[256,2048]{1,0:T(8,128)(2,1)}, u32[]{:S(2)}, u32[]{:S(2)}) collective-permute-start(bf16[256,2048]{1,0:T(8,128)(2,1)} %reduce-precision_convert_fusion.11), channel_id=1, source_target_pairs={{1,0},{2,3},{5,4},{6,7},{9,8},{10,11},{13,12},{14,15},{17,16},{18,... | collective-permute-start | bytes 3145736 | tf_op jit(solution)/shard_map/ppermute | solution.py:142
  774.3 102.7 %copy-start.4 = (bf16[2,4,8,32,768]{4,3,2,1,0:T(8,128)(2,1)S(1)}, bf16[2,4,8,32,768]{4,3,2,1,0:T(8,128)(2,1)}, u32[]{:S(2)}) copy-start(bf16[2,4,8,32,768]{4,3,2,1,0:T(8,128)(2,1)} %concatenate.117) | copy-start | bytes 9437188
  867.7 143.4 %all-to-all-start.3 = ((bf16[2,128,2048]{2,0,1:T(2,128)(2,1)}), bf16[2,128,2048]{2,0,1:T(2,128)(2,1)}, u32[]{:S(2)}, u32[]{:S(2)}) async-start(bf16[2,128,2048]{2,0,1:T(2,128)(2,1)} %copy.186), calls=%async_computation.4 | async-start | bytes 2097152 | tf_op jit(solution)/shard_map/all_to_all | solution.py:192
  872.2 6.4 copy-start.37
  1005.2 49.4 %copy-start.38 = (f32[256]{0:T(256)}, f32[256]{0:T(256)S(1)}, u32[]{:S(2)}) copy-start(f32[256]{0:T(256)S(1)} %get-tuple-element.92) | copy-start | bytes 3076
  1011.2 18.9 %all-to-all-start.8 = ((bf16[8,32,2048]{2,1,0:T(8,128)(2,1)}), bf16[8,32,2048]{2,1,0:T(8,128)(2,1)S(1)}, u32[]{:S(2)}, u32[]{:S(2)}) async-start(bf16[8,32,2048]{2,1,0:T(8,128)(2,1)} %bitcast.55), calls=%async_computation.10 | async-start | bytes 2097152 | tf_op jit(solution)/shard_map/all_to_all | solution.py:193
  1030.1 10.4 copy-start.14
  1030.1 19.7 %all-to-all-start.4 = ((bf16[8,32,2048]{2,1,0:T(8,128)(2,1)}), bf16[8,32,2048]{2,1,0:T(8,128)(2,1)}, u32[]{:S(2)}, u32[]{:S(2)}) async-start(bf16[8,32,2048]{2,1,0:T(8,128)(2,1)} %bitcast.27), calls=%async_computation.5 | async-start | bytes 2097152 | tf_op jit(solution)/shard_map/all_to_all | solution.py:193
  1040.7 14.5 %copy-start.1 = (bf16[768,2048]{1,0:T(8,128)(2,1)S(1)}, bf16[768,2048]{1,0:T(8,128)(2,1)}, u32[]{:S(2)}) copy-start(bf16[768,2048]{1,0:T(8,128)(2,1)} %param.21) | copy-start | bytes 9437188
  (5 other events, 9.0 us)
Sparse Core Ops, SparseCore 0:
  83.7 59.1 all-gather.3
  162.2 62.2 all-gather.5
  364.0 71.4 reduce-scatter.7
  439.7 78.5 reduce-scatter.5
  774.4 44.9 reduce-scatter.9
where the time goes:
time: 1070 us; the launch traced here: 1060 us
  waiting for transfers between devices  276 us (26%)
  blocking collectives  257 us (24%)
  matrix products  168 us (16%)
  other arithmetic  151 us (14%)
  starting transfers between devices  115 us (11%)
  local copies, waits for them, and re-layouts  79.8 us (7%)
  between operations  15.1 us (1%)
    ppermute x4, waiting for transfers between devices, sum_over_line(): inward = lax.ppermute(partial, 'sp', [(0, 1), (3, 2)])  180 us
    psum x1, blocking collectives, per_device(): lax.psum((vectors, bias_out, bias_qkv, bias_up), 'sp')  127 us
    all_to_all x2, waiting for transfers between devices, scatter_tokens(): part = lax.all_to_all(part, 'sp', split_axis=1, concat_axis=0, tiled=True)  89.9 us
    all_to_all x2, starting transfers between devices, scatter_tokens(): part = lax.all_to_all(part, 'sp', split_axis=1, concat_axis=0, tiled=True)  68.4 us
    all_to_all x2, blocking collectives, gather_tokens(): part = lax.all_to_all(part, 'sp', split_axis=0, concat_axis=1, tiled=True)  56.6 us
    dot_general x4, matrix products, times_transposed(): lax.dot_general(former, latter, (((1,), (1,)), ((), ())), preferred_eleme...  52 us
    dot_general x4, matrix products, times(): return jnp.dot(former, latter, preferred_element_type=jnp.float32)  49.7 us
    all_to_all x2, blocking collectives, gather_tokens(): lax.all_to_all(block, 'fsdp', split_axis=1, concat_axis=0, tiled=True)  47.4 us
  transfers between devices with their start and end apart: 23, of which 7 were waited for; matrix products, arithmetic and copies ran while one was open for 22% of the time, Pallas kernels for 0%

commit v1 on v0

--- a/solution.py
+++ b/solution.py
@@ -12,6 +12,14 @@
 ROOT_HALF = 0.7071067811865476
 ROOT_TWO_PI = 2.5066282746310002
 SCALE = 1.0 / math.sqrt(HEAD_DIM)
+
+
+def do_bars_over_axis(packet, k_dim, array_axis):
+    even = lax.axis_size("fsdp")
+    outer = jnp.split(packet, even, axis=k_dim)
+    y = jnp.stack(outer)
+    top = lax.all_to_all(y, axis_name="fsdp", split_axis=0, concat_axis=0)
+    return jnp.concatenate(top, array_axis)
 
 
 def rounded(array):
@@ -182,7 +190,7 @@
     head_sets = [[head * per_head + k for k in range(per_head)] for head in range(nf // per_head)]
 
     def gather_tokens(block):
-        part = lax.all_to_all(block, "fsdp", split_axis=1, concat_axis=0, tiled=True)
+        part = do_bars_over_axis(block, 1, 0)
         part = lax.all_to_all(part, "sp", split_axis=0, concat_axis=1, tiled=True)
         return lax.all_gather(part, "fsdp", axis=0, tiled=True).reshape(tokens, width)
 

time: 1070 us -> 1030 us (0.963)
  other arithmetic: 151 us -> 133 us
  local copies, waits for them, and re-layouts: 79.8 us -> 63.4 us
    unnamed x6 -> x5, other arithmetic: 18.4 us -> 0.22 us
    unnamed x107 -> x112, local copies, waits for them, and re-layouts: 39.6 us -> 22.5 us
    convert_element_type x9 -> x8, other arithmetic: 45 us -> 44.9 us  [rounded(): lax.reduce_precision(array.astype(jnp.float32), 8, 7).astype(jnp.bfloat16)]
  transfers between devices with their start and end apart: 23 -> 23, of which waited for: 7 -> 7; matrix products, arithmetic and copies ran while one was open for 22% -> 21% of each run, Pallas kernels for 0% -> 0%
where the time goes in v1:
time: 1030 us; the launch traced here: 1020 us
  waiting for transfers between devices  276 us (27%)
  blocking collectives  254 us (25%)
  matrix products  170 us (17%)
  other arithmetic  133 us (13%)
  starting transfers between devices  112 us (11%)
  local copies, waits for them, and re-layouts  63.4 us (6%)
  between operations  15.2 us (1%)
    ppermute x4, waiting for transfers between devices, sum_over_line(): inward = lax.ppermute(partial, 'sp', [(0, 1), (3, 2)])  180 us
    psum x1, blocking collectives, per_device(): lax.psum((vectors, bias_out, bias_qkv, bias_up), 'sp')  127 us
    all_to_all x2, waiting for transfers between devices, scatter_tokens(): part = lax.all_to_all(part, 'sp', split_axis=1, concat_axis=0, tiled=True)  90.2 us
    all_to_all x2, starting transfers between devices, scatter_tokens(): part = lax.all_to_all(part, 'sp', split_axis=1, concat_axis=0, tiled=True)  68.4 us
    all_to_all x2, blocking collectives, gather_tokens(): part = lax.all_to_all(part, 'sp', split_axis=0, concat_axis=1, tiled=True)  58.7 us
    dot_general x4, matrix products, times_transposed(): lax.dot_general(former, latter, (((1,), (1,)), ((), ())), preferred_eleme...  51.7 us
    dot_general x4, matrix products, times(): return jnp.dot(former, latter, preferred_element_type=jnp.float32)  49.7 us
    convert_element_type x8, other arithmetic, rounded(): lax.reduce_precision(array.astype(jnp.float32), 8, 7).astype(jnp.bfloat16)  44.9 us
  transfers between devices with their start and end apart: 23, of which 7 were waited for; matrix products, arithmetic and copies ran while one was open for 21% of the time, Pallas kernels for 0%

profile of v1, /device:TPU:0, one launch (start us, length us, event | category | flops | bytes accessed | tf_op | source)
XLA Modules:
  0.0 1023.4 jit_solution(12187405230505349408)
XLA Ops:
  14.8 20.3 %all_to_all.132 = bf16[8,1,32,2048]{3,2,1,0:T(8,128)(2,1)S(1)} all-to-all(bf16[8,1,32,2048]{3,2,1,0:T(8,128)(2,1)S(1)} %bitcast_dynamic-update-slice_fusion.8), channel_id=1, replica_groups=mesh['fsdp'=8,'sp'=4] {'fsdp'}, dimensions={0} | all-to-all | bytes 2097152 | tf_op jit(solution)/shard_map/all_to_all | solution.py:21
  35.1 29.8 %all_to_all.133 = bf16[8,32,2048]{2,1,0:T(8,128)(2,1)S(1)} all-to-all(bf16[8,32,2048]{2,1,0:T(8,128)(2,1)S(1)} %bitcast.219), channel_id=1, replica_groups=mesh['fsdp'=8,'sp'=4] {'sp'}, dimensions={0} | all-to-all | bytes 2097152 | tf_op jit(solution)/shard_map/all_to_all | solution.py:194
  73.4 24.5 %all_to_all.134 = bf16[8,1,32,2048]{3,2,1,0:T(8,128)(2,1)S(1)} all-to-all(bf16[8,1,32,2048]{3,2,1,0:T(8,128)(2,1)S(1)} %bitcast_dynamic-update-slice_fusion), channel_id=1, replica_groups=mesh['fsdp'=8,'sp'=4] {'fsdp'}, dimensions={0} | all-to-all | bytes 2097152 | tf_op jit(solution)/shard_map/all_to_all | solution.py:21
  97.9 28.9 %all_to_all.135 = bf16[8,32,2048]{2,1,0:T(8,128)(2,1)S(1)} all-to-all(bf16[8,32,2048]{2,1,0:T(8,128)(2,1)S(1)} %bitcast.221), channel_id=1, replica_groups=mesh['fsdp'=8,'sp'=4] {'sp'}, dimensions={0} | all-to-all | bytes 2097152 | tf_op jit(solution)/shard_map/all_to_all | solution.py:194
  130.2 4.2 all-to-all-start.2
  134.5 23.7 %all-gather = s32[8,1,1024]{2,1,0:T(1,128)S(1)} all-gather(s32[1,1,1024]{2,1,0:T(1,128)S(1)} %bitcast.250), channel_id=1, replica_groups=mesh['fsdp'=8,'sp'=4] {'fsdp'}, dimensions={0}, use_global_device_ids=true | all-gather | bytes 36864 | tf_op jit(solution)/shard_map/all_gather | solution.py:228
  166.2 4.7 convert_reduce_fusion.1
  175.0 7.4 add_convert_fusion.2
  182.3 7.1 add_convert_fusion.3
  194.4 6.1 convolution_convert_fusion.1
  201.8 4.9 fusion.42
  206.7 3.2 fusion.9
  209.9 3.3 fusion.8
  213.3 4.9 fusion.28
  218.2 5.1 multiply_reduce_fusion.3
  223.3 3.7 multiply_convert_fusion
  227.0 2.8 multiply_bitcast_fusion
  235.0 4.6 slice_multiply_fusion.2
  246.0 5.0 fusion.38
  250.9 7.0 concatenate.117
  258.0 3.9 copy.187
  261.9 15.3 %multiply_convert_fusion.1 = (bf16[2048,1024]{1,0:T(8,128)(2,1)}, f32[2048,1024]{1,0:T(8,128)}) fusion(f32[1024]{0:T(1024)S(1)} %dynamic_slice.14, bf16[2048,2048]{1,0:T(8,128)(2,1)} %get-tuple-element.26, bf16[1024,2048]{1,0:T(8,128)(2,1)S(1)} %copy-done.39), kind=kOutput, calls=%fused_computation.29 | convolution fusion | flops 8602517504 | bytes 25169920 | tf_op jit(solution)/shard_map/dot_general | solution.py:36
  277.3 17.5 %convert_reduce_fusion.2 = (f32[1024]{0:T(1024)}, bf16[2048,1024]{1,0:T(8,128)(2,1)}) fusion(f32[2048,1024]{1,0:T(8,128)} %get-tuple-element.60, f32[1024]{0:T(1024)S(1)} %dynamic_slice.14, bf16[2048,2048]{1,0:T(8,128)(2,1)S(1)} %bitcast.205, bf16[1024,2048]{1,0:T(8,128)(2,1)} %param.27), kind=kOutput, calls=%fused_computation.22 | convolution fusion | flops 8617196544 | bytes 25174016 | tf_op jit(solution)/shard_map/dot_general | solution.py:36
  294.8 14.1 %fusion.60 = f32[2048,2048]{1,0:T(8,128)} fusion(bf16[2048,1024]{1,0:T(8,128)(2,1)} %get-tuple-element.62, bf16[1024,2048]{1,0:T(8,128)(2,1)S(1)} %copy-done.39), kind=kOutput, calls=%fused_computation.162 | convolution fusion | flops 8589934592 | bytes 25165824 | tf_op jit(solution)/shard_map/dot_general | solution.py:42
  308.9 17.8 %multiply_reduce_fusion.1 = (f32[2048]{0:T(1024)S(1)}, f32[2048]{0:T(1024)S(1)}, f32[2048]{0:T(1024)S(1)}, f32[2048]{0:T(1024)S(1)}, bf16[2048,2048]{1,0:T(8,128)(2,1)}) fusion(bf16[16,128,2048]{2,1,0:T(8,128)(2,1)} %all-gather.4.cloned.1.call-done, f32[2048]{0:T(1024)S(1)} %get-tuple-element.48, f32[2048]{0:T(1024)S(1)} %get-tuple-element.49, ...), kind=kOutput, calls=%fused_computation.5 | convolution fusion | flops 6501163008 | bytes 39911424 | tf_op jit(solution)/shard_map/dot_general | solution.py:42
  327.9 8.2 fusion.31
  337.3 15.2 %reduce-precision_convert_fusion.7 = bf16[1024,2048]{1,0:T(8,128)(2,1)} fusion(bf16[2048,1024]{1,0:T(8,128)(2,1)} %get-tuple-element.62, bf16[2048,2048]{1,0:T(8,128)(2,1)} %get-tuple-element.26), kind=kOutput, calls=%fused_computation.25 | convolution fusion | flops 8594128896 | bytes 16777216 | tf_op jit(solution)/shard_map/dot_general | solution.py:30
  352.5 3.4 collective-permute-start.6
  355.9 11.7 %fusion.59 = f32[2048,2048]{1,0:T(8,128)} fusion(bf16[2048,1024]{1,0:T(8,128)(2,1)S(1)} %copy-done.41, bf16[1024,2048]{1,0:T(8,128)(2,1)S(1)} %copy-done.40), kind=kOutput, calls=%fused_computation.161 | convolution fusion | flops 8589934592 | bytes 25165824 | tf_op jit(solution)/shard_map/dot_general | solution.py:42
  367.7 11.7 %reduce-precision_convert_fusion.1 = bf16[2048,2048]{1,0:T(8,128)(2,1)} fusion(f32[2048,2048]{1,0:T(8,128)} %fusion.59, bf16[2048,256]{1,0:T(8,128)(2,1)S(1)} %bitcast.228, bf16[2048,256]{1,0:T(8,128)(2,1)S(1)} %bitcast.227), kind=kOutput, calls=%fused_computation.7 | convolution fusion | flops 2160066560 | bytes 27262976 | tf_op jit(solution)/shard_map/dot_general | solution.py:36
  379.4 14.7 %reduce-precision_convert_fusion.4 = bf16[1024,2048]{1,0:T(8,128)(2,1)} fusion(bf16[2048,1024]{1,0:T(8,128)(2,1)} %get-tuple-element.59, bf16[2048,2048]{1,0:T(8,128)(2,1)} %bitcast.202), kind=kOutput, calls=%fused_computation.21 | convolution fusion | flops 8594128896 | bytes 16777216 | tf_op jit(solution)/shard_map/dot_general | solution.py:30
  394.1 3.3 collective-permute-start.9
  397.4 6.3 add_convert_fusion
  403.7 8.3 reduce-precision_convert_fusion.10
  412.0 3.0 collective-permute-start
  415.0 30.1 %collective-permute-done.6 = bf16[1024,2048]{1,0:T(8,128)(2,1)} collective-permute-done((bf16[1024,2048]{1,0:T(8,128)(2,1)}, bf16[1024,2048]{1,0:T(8,128)(2,1)}, u32[]{:S(2)}, u32[]{:S(2)}) %collective-permute-start.6) | collective-permute-done | bytes 4194336 | tf_op jit(solution)/shard_map/ppermute | solution.py:146
  445.1 7.8 reduce-precision_convert_fusion.6
  452.9 2.7 collective-permute-start.7
  455.6 3.6 convolution_convert_fusion
  459.3 3.6 all-to-all-start.9
  462.8 72.1 %collective-permute-done.9 = bf16[1024,2048]{1,0:T(8,128)(2,1)} collective-permute-done((bf16[1024,2048]{1,0:T(8,128)(2,1)}, bf16[1024,2048]{1,0:T(8,128)(2,1)}, u32[]{:S(2)}, u32[]{:S(2)}) %collective-permute-start.9) | collective-permute-done | bytes 4194336 | tf_op jit(solution)/shard_map/ppermute | solution.py:146
  535.0 7.7 reduce-precision_convert_fusion.3
  542.7 2.8 collective-permute-start.10
  545.5 56.5 %collective-permute-done = bf16[768,2048]{1,0:T(8,128)(2,1)} collective-permute-done((bf16[768,2048]{1,0:T(8,128)(2,1)}, bf16[768,2048]{1,0:T(8,128)(2,1)}, u32[]{:S(2)}, u32[]{:S(2)}) %collective-permute-start) | collective-permute-done | bytes 3145760 | tf_op jit(solution)/shard_map/ppermute | solution.py:146
  602.0 6.1 reduce-precision_convert_fusion.9
  610.8 4.1 collective-permute-start.3
  615.6 21.6 %collective-permute-done.3 = bf16[256,2048]{1,0:T(8,128)(2,1)S(1)} collective-permute-done((bf16[256,2048]{1,0:T(8,128)(2,1)S(1)}, bf16[256,2048]{1,0:T(8,128)(2,1)S(1)}, u32[]{:S(2)}, u32[]{:S(2)}) %collective-permute-start.3) | collective-permute-done | bytes 1048608 | tf_op jit(solution)/shard_map/ppermute | solution.py:146
  638.3 7.7 reduce-precision_convert_fusion.5
  647.3 6.1 reduce-precision_convert_fusion.8
  654.7 3.3 copy.188
  658.0 64.0 %all-to-all-start.7 = ((bf16[2,128,2048]{2,0,1:T(2,128)(2,1)}), bf16[2,128,2048]{2,0,1:T(2,128)(2,1)}, u32[]{:S(2)}, u32[]{:S(2)}) async-start(bf16[2,128,2048]{2,0,1:T(2,128)(2,1)} %copy.188), calls=%async_computation.9 | async-start | bytes 2097152 | tf_op jit(solution)/shard_map/all_to_all | solution.py:200
  722.0 7.7 reduce-precision_convert_fusion.2
  735.2 3.4 copy.173
  738.6 90.2 %all-to-all-done.7 = bf16[2,128,2048]{2,0,1:T(2,128)(2,1)} async-done(((bf16[2,128,2048]{2,0,1:T(2,128)(2,1)}), bf16[2,128,2048]{2,0,1:T(2,128)(2,1)}, u32[]{:S(2)}, u32[]{:S(2)}) %all-to-all-start.7) | async-done | bytes 1048608 | tf_op jit(solution)/shard_map/all_to_all | solution.py:200
  828.8 4.5 all-to-all-start.3
  833.3 4.7 convert_reduce_fusion
  839.6 126.8 %all-reduce.1 = (f32[256,4]{0,1:T(4,128)S(1)}, f32[768]{0:T(1024)}, f32[256]{0:T(256)S(1)}, f32[1024]{0:T(1024)}) all-reduce(f32[256,4]{0,1:T(4,128)S(1)} %copy.203, f32[768]{0:T(1024)S(1)} %convert_reduce_fusion.3, f32[256]{0:T(256)S(1)} %dynamic_slice.15, f32[1024]{0:T(1024)S(1)} %copy-done.37), channel_id=1, replica_groups=mesh['fsdp'=8,'sp'=4] {'sp'}, use_global_device_ids=true, to_apply=%region_18.19 | all-reduce | flops 3072 | bytes 24576 | tf_op jit(solution)/shard_map/psum | solution.py:292
  972.4 3.6 all-to-all-start.8
  976.0 5.0 select_convert_fusion.2
  981.0 6.1 select_convert_fusion.1
  991.3 4.2 all-to-all-start.4
  995.6 6.1 select_convert_fusion
  1006.7 4.2 all-to-all-done.4
  1011.0 4.9 fusion.21
  (206 shorter events, 81.1 us)
Async XLA Ops:
  7.2 175.2 %copy-start = (bf16[768,2048]{1,0:T(8,128)(2,1)S(1)}, bf16[768,2048]{1,0:T(8,128)(2,1)}, u32[]{:S(2)}) copy-start(bf16[768,2048]{1,0:T(8,128)(2,1)} %param.21) | copy-start | bytes 9437188
  7.2 159.0 %all-gather.4.cloned.1.call-start = ((), (), s32[]{:S(2)}) async-start(), calls=%async_computation.13 | async-start | bytes 9437184 | tf_op jit(solution)/shard_map/all_gather | solution.py:195
  65.9 128.5 %all-gather.6.cloned.1.call-start = ((), (), s32[]{:S(2)}) async-start(), calls=%async_computation.15 | async-start | bytes 9437184 | tf_op jit(solution)/shard_map/all_gather | solution.py:195
  69.6 64.9 %copy-start.36 = (s32[1,1024]{1,0:T(1,128)S(1)}, s32[1,1024]{1,0:T(1,128)}, u32[]{:S(2)}) copy-start(s32[1,1024]{1,0:T(1,128)} %param.16) | copy-start | bytes 12292
  130.2 33.4 %all-to-all-start.2 = ((bf16[256,8,256]{0,2,1:T(8,128)(2,1)}), bf16[256,8,256]{0,2,1:T(8,128)(2,1)}, u32[]{:S(2)}, u32[]{:S(2)}) async-start(bf16[256,8,256]{0,2,1:T(8,128)(2,1)} %bitcast.218), calls=%async_computation.2 | async-start | bytes 2097152 | tf_op jit(solution)/shard_map/all_to_all | solution.py:230
  134.5 520.3 %reduce-scatter.8.cloned.1.call-start = ((), (), s32[]{:S(2)}) async-start(), calls=%async_computation.16 | async-start | bytes 9437184 | tf_op jit(solution)/shard_map/reduce_scatter | solution.py:199
  166.2 5.8 copy-start.2
  170.9 4.1 copy-start.28
  170.9 4.1 copy-start.30
  170.9 4.1 copy-start.32
  170.9 4.1 copy-start.33
  170.9 11.4 %copy-start.26 = (f32[16,128]{1,0:T(8,128)}, f32[16,128]{1,0:T(8,128)S(1)}, u32[]{:S(2)}) copy-start(f32[16,128]{1,0:T(8,128)S(1)} %get-tuple-element.50) | copy-start | bytes 24580
  194.4 6.2 copy-start.12
  194.4 6.2 copy-start.13
  201.3 5.3 copy-start.15
  201.4 5.3 copy-start.19
  201.4 5.3 copy-start.24
  206.7 3.2 copy-start.22
  206.7 3.2 copy-start.25
  209.9 13.4 %copy-start.3 = (f32[2,1024,1024]{1,2,0:T(8,128)}, f32[2,1024,1024]{1,2,0:T(8,128)S(1)}, u32[]{:S(2)}) copy-start(f32[2,1024,1024]{1,2,0:T(8,128)S(1)} %get-tuple-element.56) | copy-start | bytes 25165828
  229.8 5.1 copy-start.17
  232.0 3.0 copy-start.10
  241.9 4.1 copy-start.9
  241.9 4.1 copy-start.11
  241.9 4.1 copy-start.18
  258.0 4.0 copy-start.39
  258.0 19.3 %slice-start = ((s8[8388608]{0:T(1024)(128)(4,1)}), s8[4194304]{0:T(1024)(128)(4,1)S(1)}, s32[]{:S(2)}) async-start(s8[8388608]{0:T(1024)(128)(4,1)} %bitcast.203), calls=%async_computation.18 | async-start | bytes 8388608
  261.9 15.3 %slice-start.1 = ((s8[8388608]{0:T(1024)(128)(4,1)}), s8[4194304]{0:T(1024)(128)(4,1)S(1)}, s32[]{:S(2)}) async-start(s8[8388608]{0:T(1024)(128)(4,1)} %bitcast.203), calls=%async_computation.19 | async-start | bytes 8388608
  326.7 408.4 %reduce-scatter.6.cloned.1.call-start = ((), (), s32[]{:S(2)}) async-start(), calls=%async_computation.14 | async-start | bytes 9437184 | tf_op jit(solution)/shard_map/reduce_scatter | solution.py:199
  337.3 18.7 %copy-start.40 = (bf16[1024,2048]{1,0:T(8,128)(2,1)S(1)}, bf16[1024,2048]{1,0:T(8,128)(2,1)}, u32[]{:S(2)}) copy-start(bf16[1024,2048]{1,0:T(8,128)(2,1)} %param.27) | copy-start | bytes 12582916
  337.3 18.7 %copy-start.41 = (bf16[2048,1024]{1,0:T(8,128)(2,1)S(1)}, bf16[2048,1024]{1,0:T(8,128)(2,1)}, u32[]{:S(2)}) copy-start(bf16[2048,1024]{1,0:T(8,128)(2,1)} %get-tuple-element.59) | copy-start | bytes 12582916
  352.5 92.6 %collective-permute-start.6 = (bf16[1024,2048]{1,0:T(8,128)(2,1)}, bf16[1024,2048]{1,0:T(8,128)(2,1)}, u32[]{:S(2)}, u32[]{:S(2)}) collective-permute-start(bf16[1024,2048]{1,0:T(8,128)(2,1)} %reduce-precision_convert_fusion.7), channel_id=1, source_target_pairs={{0,1},{3,2},{4,5},{7,6},{8,9},{11,10},{12,13},{15,14},{16,17},{19,... | collective-permute-start | bytes 12582920 | tf_op jit(solution)/shard_map/ppermute | solution.py:146
  355.9 11.7 %copy-start.20 = (bf16[8,256,256]{2,1,0:T(8,128)(2,1)S(1)}, bf16[8,256,256]{2,1,0:T(8,128)(2,1)}, u32[]{:S(2)}) copy-start(bf16[8,256,256]{2,1,0:T(8,128)(2,1)} %copy.172) | copy-start | bytes 3145732
  379.4 18.0 %copy-start.27 = (f32[16,128]{1,0:T(8,128)S(1)}, f32[16,128]{1,0:T(8,128)}, u32[]{:S(2)}) copy-start(f32[16,128]{1,0:T(8,128)} %copy-done.26) | copy-start | bytes 24580
  379.4 18.0 %copy-start.29 = (f32[2048]{0:T(1024)S(1)}, f32[2048]{0:T(1024)}, u32[]{:S(2)}) copy-start(f32[2048]{0:T(1024)} %param.18) | copy-start | bytes 24580
  379.4 18.0 %copy-start.31 = (f32[16,128]{1,0:T(8,128)S(1)}, f32[16,128]{1,0:T(8,128)}, u32[]{:S(2)}) copy-start(f32[16,128]{1,0:T(8,128)} %get-tuple-element.47) | copy-start | bytes 24580
  394.1 140.9 %collective-permute-start.9 = (bf16[1024,2048]{1,0:T(8,128)(2,1)}, bf16[1024,2048]{1,0:T(8,128)(2,1)}, u32[]{:S(2)}, u32[]{:S(2)}) collective-permute-start(bf16[1024,2048]{1,0:T(8,128)(2,1)} %reduce-precision_convert_fusion.4), channel_id=1, source_target_pairs={{0,1},{3,2},{4,5},{7,6},{8,9},{11,10},{12,13},{15,14},{16,17},{19,... | collective-permute-start | bytes 12582920 | tf_op jit(solution)/shard_map/ppermute | solution.py:146
  397.4 6.3 copy-start.21
  403.7 52.0 %slice-start.2 = ((s8[8388608]{0:T(1024)(128)(4,1)}), s8[4194304]{0:T(1024)(128)(4,1)S(1)}, s32[]{:S(2)}) async-start(s8[8388608]{0:T(1024)(128)(4,1)} %bitcast.206), calls=%async_computation.20 | async-start | bytes 8388608
  403.7 52.0 %slice-start.3 = ((s8[8388608]{0:T(1024)(128)(4,1)}), s8[4194304]{0:T(1024)(128)(4,1)S(1)}, s32[]{:S(2)}) async-start(s8[8388608]{0:T(1024)(128)(4,1)} %bitcast.206), calls=%async_computation.21 | async-start | bytes 8388608
  412.0 190.0 %collective-permute-start = (bf16[768,2048]{1,0:T(8,128)(2,1)}, bf16[768,2048]{1,0:T(8,128)(2,1)}, u32[]{:S(2)}, u32[]{:S(2)}) collective-permute-start(bf16[768,2048]{1,0:T(8,128)(2,1)} %reduce-precision_convert_fusion.10), channel_id=1, source_target_pairs={{0,1},{3,2},{4,5},{7,6},{8,9},{11,10},{12,13},{15,14},{16,17},{19,... | collective-permute-start | bytes 9437192 | tf_op jit(solution)/shard_map/ppermute | solution.py:146
  452.9 185.3 %collective-permute-start.7 = (bf16[1024,2048]{1,0:T(8,128)(2,1)}, bf16[1024,2048]{1,0:T(8,128)(2,1)}, u32[]{:S(2)}, u32[]{:S(2)}) collective-permute-start(bf16[1024,2048]{1,0:T(8,128)(2,1)} %reduce-precision_convert_fusion.6), channel_id=1, source_target_pairs={{1,2},{2,1},{5,6},{6,5},{9,10},{10,9},{13,14},{14,13},{17,18},{18,... | collective-permute-start | bytes 12582920 | tf_op jit(solution)/shard_map/ppermute | solution.py:148
  459.3 151.3 %all-to-all-start.9 = ((bf16[8,256,256]{2,1,0:T(8,128)(2,1)}), bf16[8,256,256]{2,1,0:T(8,128)(2,1)S(1)}, u32[]{:S(2)}, u32[]{:S(2)}) async-start(bf16[8,256,256]{2,1,0:T(8,128)(2,1)} %bitcast.84), calls=%async_computation.11 | async-start | bytes 2097152 | tf_op jit(solution)/shard_map/all_to_all | solution.py:278
  542.7 72.3 %copy-start.5 = (bf16[1,256,2048]{2,1,0:T(8,128)(2,1)S(1)}, bf16[1,256,2048]{2,1,0:T(8,128)(2,1)}, u32[]{:S(2)}) copy-start(bf16[1,256,2048]{2,1,0:T(8,128)(2,1)} %param.15) | copy-start | bytes 3145732
  542.7 179.4 %collective-permute-start.10 = (bf16[1024,2048]{1,0:T(8,128)(2,1)}, bf16[1024,2048]{1,0:T(8,128)(2,1)}, u32[]{:S(2)}, u32[]{:S(2)}) collective-permute-start(bf16[1024,2048]{1,0:T(8,128)(2,1)} %reduce-precision_convert_fusion.3), channel_id=1, source_target_pairs={{1,2},{2,1},{5,6},{6,5},{9,10},{10,9},{13,14},{14,13},{17,18},{18,... | collective-permute-start | bytes 12582920 | tf_op jit(solution)/shard_map/ppermute | solution.py:148
  608.1 39.2 %collective-permute-start.1 = (bf16[768,2048]{1,0:T(8,128)(2,1)}, bf16[768,2048]{1,0:T(8,128)(2,1)}, u32[]{:S(2)}, u32[]{:S(2)}) collective-permute-start(bf16[768,2048]{1,0:T(8,128)(2,1)} %reduce-precision_convert_fusion.9), channel_id=1, source_target_pairs={{1,2},{2,1},{5,6},{6,5},{9,10},{10,9},{13,14},{14,13},{17,18},{18,... | collective-permute-start | bytes 9437192 | tf_op jit(solution)/shard_map/ppermute | solution.py:148
  610.8 26.3 %collective-permute-start.3 = (bf16[256,2048]{1,0:T(8,128)(2,1)S(1)}, bf16[256,2048]{1,0:T(8,128)(2,1)S(1)}, u32[]{:S(2)}, u32[]{:S(2)}) collective-permute-start(bf16[256,2048]{1,0:T(8,128)(2,1)S(1)} %bitcast.214), channel_id=1, source_target_pairs={{0,1},{3,2},{4,5},{7,6},{8,9},{11,10},{12,13},{15,14},{16,17},{19,... | collective-permute-start | bytes 3145736 | tf_op jit(solution)/shard_map/ppermute | solution.py:146
  637.5 93.5 %collective-permute-start.4 = (bf16[256,2048]{1,0:T(8,128)(2,1)S(1)}, bf16[256,2048]{1,0:T(8,128)(2,1)S(1)}, u32[]{:S(2)}, u32[]{:S(2)}) collective-permute-start(bf16[256,2048]{1,0:T(8,128)(2,1)S(1)} %reduce-precision_convert_fusion.12), channel_id=1, source_target_pairs={{1,2},{2,1},{5,6},{6,5},{9,10},{10,9},{13,14},{14,13},{17,18},{18,... | collective-permute-start | bytes 3145736 | tf_op jit(solution)/shard_map/ppermute | solution.py:148
  646.0 335.0 %collective-permute-start.8 = (bf16[1024,2048]{1,0:T(8,128)(2,1)}, bf16[1024,2048]{1,0:T(8,128)(2,1)}, u32[]{:S(2)}, u32[]{:S(2)}) collective-permute-start(bf16[1024,2048]{1,0:T(8,128)(2,1)} %reduce-precision_convert_fusion.5), channel_id=1, source_target_pairs={{1,0},{2,3},{5,4},{6,7},{9,8},{10,11},{13,12},{14,15},{17,16},{18,... | collective-permute-start | bytes 12582920 | tf_op jit(solution)/shard_map/ppermute | solution.py:150
  653.4 322.5 %collective-permute-start.2 = (bf16[768,2048]{1,0:T(8,128)(2,1)}, bf16[768,2048]{1,0:T(8,128)(2,1)}, u32[]{:S(2)}, u32[]{:S(2)}) collective-permute-start(bf16[768,2048]{1,0:T(8,128)(2,1)} %reduce-precision_convert_fusion.8), channel_id=1, source_target_pairs={{1,0},{2,3},{5,4},{6,7},{9,8},{10,11},{13,12},{14,15},{17,16},{18,... | collective-permute-start | bytes 9437192 | tf_op jit(solution)/shard_map/ppermute | solution.py:150
  658.0 170.7 %all-to-all-start.7 = ((bf16[2,128,2048]{2,0,1:T(2,128)(2,1)}), bf16[2,128,2048]{2,0,1:T(2,128)(2,1)}, u32[]{:S(2)}, u32[]{:S(2)}) async-start(bf16[2,128,2048]{2,0,1:T(2,128)(2,1)} %copy.188), calls=%async_computation.9 | async-start | bytes 2097152 | tf_op jit(solution)/shard_map/all_to_all | solution.py:200
  722.0 9.0 copy-start.34
  722.0 9.0 copy-start.35
  722.0 116.7 %reduce-scatter.10.cloned.1.call-start = ((), (), s32[]{:S(2)}) async-start(), calls=%async_computation.17 | async-start | bytes 1179648
  729.7 265.8 %collective-permute-start.11 = (bf16[1024,2048]{1,0:T(8,128)(2,1)}, bf16[1024,2048]{1,0:T(8,128)(2,1)}, u32[]{:S(2)}, u32[]{:S(2)}) collective-permute-start(bf16[1024,2048]{1,0:T(8,128)(2,1)} %reduce-precision_convert_fusion.2), channel_id=1, source_target_pairs={{1,0},{2,3},{5,4},{6,7},{9,8},{10,11},{13,12},{14,15},{17,16},{18,... | collective-permute-start | bytes 12582920 | tf_op jit(solution)/shard_map/ppermute | solution.py:150
  732.4 234.6 %collective-permute-start.5 = (bf16[256,2048]{1,0:T(8,128)(2,1)}, bf16[256,2048]{1,0:T(8,128)(2,1)}, u32[]{:S(2)}, u32[]{:S(2)}) collective-permute-start(bf16[256,2048]{1,0:T(8,128)(2,1)} %reduce-precision_convert_fusion.11), channel_id=1, source_target_pairs={{1,0},{2,3},{5,4},{6,7},{9,8},{10,11},{13,12},{14,15},{17,16},{18,... | collective-permute-start | bytes 3145736 | tf_op jit(solution)/shard_map/ppermute | solution.py:150
  735.1 102.9 %copy-start.4 = (bf16[2,4,8,32,768]{4,3,2,1,0:T(8,128)(2,1)S(1)}, bf16[2,4,8,32,768]{4,3,2,1,0:T(8,128)(2,1)}, u32[]{:S(2)}) copy-start(bf16[2,4,8,32,768]{4,3,2,1,0:T(8,128)(2,1)} %concatenate.117) | copy-start | bytes 9437188
  828.8 143.6 %all-to-all-start.3 = ((bf16[2,128,2048]{2,0,1:T(2,128)(2,1)}), bf16[2,128,2048]{2,0,1:T(2,128)(2,1)}, u32[]{:S(2)}, u32[]{:S(2)}) async-start(bf16[2,128,2048]{2,0,1:T(2,128)(2,1)} %copy.173), calls=%async_computation.4 | async-start | bytes 2097152 | tf_op jit(solution)/shard_map/all_to_all | solution.py:200
  833.2 6.4 copy-start.37
  966.4 49.4 %copy-start.38 = (f32[256]{0:T(256)}, f32[256]{0:T(256)S(1)}, u32[]{:S(2)}) copy-start(f32[256]{0:T(256)S(1)} %get-tuple-element.92) | copy-start | bytes 3076
  972.4 18.9 %all-to-all-start.8 = ((bf16[8,32,2048]{2,1,0:T(8,128)(2,1)}), bf16[8,32,2048]{2,1,0:T(8,128)(2,1)S(1)}, u32[]{:S(2)}, u32[]{:S(2)}) async-start(bf16[8,32,2048]{2,1,0:T(8,128)(2,1)} %bitcast.73), calls=%async_computation.10 | async-start | bytes 2097152 | tf_op jit(solution)/shard_map/all_to_all | solution.py:201
  991.3 10.4 %copy-start.14 = (bf16[8,32,2048]{2,1,0:T(8,128)(2,1)}, bf16[8,32,2048]{2,1,0:T(8,128)(2,1)S(1)}, u32[]{:S(2)}) copy-start(bf16[8,32,2048]{2,1,0:T(8,128)(2,1)S(1)} %all-to-all-done.8) | copy-start | bytes 3145732
  991.3 19.7 %all-to-all-start.4 = ((bf16[8,32,2048]{2,1,0:T(8,128)(2,1)}), bf16[8,32,2048]{2,1,0:T(8,128)(2,1)}, u32[]{:S(2)}, u32[]{:S(2)}) async-start(bf16[8,32,2048]{2,1,0:T(8,128)(2,1)} %bitcast.36), calls=%async_computation.5 | async-start | bytes 2097152 | tf_op jit(solution)/shard_map/all_to_all | solution.py:201
  1001.9 14.5 %copy-start.1 = (bf16[768,2048]{1,0:T(8,128)(2,1)S(1)}, bf16[768,2048]{1,0:T(8,128)(2,1)}, u32[]{:S(2)}) copy-start(bf16[768,2048]{1,0:T(8,128)(2,1)} %param.21) | copy-start | bytes 9437188
  (5 other events, 9.0 us)
Sparse Core Ops, SparseCore 0:
  66.0 63.5 all-gather.3
  132.1 58.3 all-gather.5
  326.9 69.0 reduce-scatter.7
  400.2 78.0 reduce-scatter.5
  735.3 45.1 reduce-scatter.9
